TPU v7x, 32 devices: a whole 2x2x4 slice. The times are simulated.
32 devices in a mesh: group: 2 (over y), seq: 4 (over z), mp: 4 (over x, core).
Axes of the slice: x: 2, y: 2, z: 4, core: 2. Of those that a mesh axis runs over, the one named last changes fastest.
Arguments:
- embeds: bfloat16 [8192, 8192], P('seq', 'mp'), may hold values from -250 to 250
- image_feats: bfloat16 [512, 7296], P('seq'), may hold values from -6 to 6
- image_pos: int32 [512], P('seq'), may hold values from 0 to 8191, as said below
- proj_w: bfloat16 [7296, 8192], P('seq', 'mp'), may hold values from -0.0625 to 0.0625
- proj_b: bfloat16 [8192], P('mp'), may hold values from -3 to 3
- norm_gain: bfloat16 [8192], P('mp'), may hold values from 0.099609375 to 1.8984375
- kv_w: bfloat16 [8192, 2048], P('mp'), may hold values from -0.0625 to 0.0625
- prompt_lengths: int32 [2], replicated, may hold values from 2048 to 4096
- page_owner: int32 [512, 1], P('seq'), may hold values from 0 to 3; in each aligned block of 128 rows (0 to 127, 128 to 255, ...) at most 64 rows name the same one
- queries: bfloat16 [512, 8192], P('seq', 'mp'), may hold values from -180 to 180
- kv_cache: bfloat16 [512, 128, 2048], P('seq', None, 'mp'), may hold values from -5 to 5
- new_kv: bfloat16 [512, 2048], P('seq', 'mp'), may hold values from -5 to 5
- cache_lengths: int32 [512], P('seq'), may hold values from 2 to 128
Outputs:
- page_slots: bfloat16 [2048, 16, 2048], P(('group', 'seq'), None, 'mp')
- row_states: bfloat16 [1024, 8192], P(('group', 'seq'), 'mp')
Inputs may be any that keep to these rules, and one draw needn't show every extreme that they name: `image_pos`: distinct and increasing; entries s * 128 to (s + 1) * 128 - 1 lie among tokens s * 2048 to (s + 1) * 2048 - 1. `page_owner`: among the 128 pages of one seq index no owner is named more than 64 times.
All inputs are finite; a program needn't handle non-finite values.
Results may differ from a plain program's by a relative error of at most 0.005.
Values may be sent and summed in bfloat16 or wider, within the bound.
A program may use at most 128 MiB of HBM per device.

v0:
```python
import jax
import jax.numpy as jnp
from jax import lax
from jax.sharding import PartitionSpec as P

D = 8192
HEAD = 128
PAGE = 16
PROMPT_LEN = 4096


def gated(condition, action, empty_value, *operands):
    return lax.cond(condition, action, lambda *unused: empty_value, *operands)


def attend(queries, kv_cache, new_kv, cache_lengths):
    row_count = queries.shape[0]
    heads_kv = kv_cache.shape[2] // (2 * HEAD)
    grouped = queries.reshape(row_count, heads_kv, queries.shape[1] // (HEAD * heads_kv), HEAD)
    stored = kv_cache.reshape(row_count, kv_cache.shape[1], heads_kv, 2 * HEAD)
    fresh_kv = new_kv.reshape(row_count, heads_kv, 2 * HEAD)
    scores = jnp.einsum(
        "rgqh,rjgh->rgqj", grouped, stored[..., :HEAD], preferred_element_type=jnp.float32
    ) * HEAD ** (-0.5)
    in_cache = jnp.arange(stored.shape[1], dtype=jnp.int32)[None, :] < cache_lengths[:, None]
    scores = jnp.where(in_cache[:, None, None, :], scores, -1e30)
    own_score = jnp.einsum(
        "rgqh,rgh->rgq", grouped, fresh_kv[..., :HEAD], preferred_element_type=jnp.float32
    ) * HEAD ** (-0.5)
    row_max = jnp.maximum(jnp.max(scores, axis=3), own_score)
    weights = jnp.exp(scores - row_max[..., None])
    own_weight = jnp.exp(own_score - row_max)
    denominator = jnp.sum(weights, axis=3) + own_weight
    probability = (weights / denominator[..., None]).astype(jnp.bfloat16)
    own_prob = lax.optimization_barrier((own_weight / denominator).astype(jnp.bfloat16)).astype(
        jnp.float32
    )
    attended = jnp.einsum(
        "rgqj,rjgh->rgqh", probability, stored[..., HEAD:], preferred_element_type=jnp.float32
    )
    attended = attended + own_prob[..., None] * fresh_kv[:, :, None, HEAD:].astype(jnp.float32)
    return attended.astype(jnp.bfloat16).reshape(row_count, queries.shape[1])


def per_device(
    embeds,
    image_feats,
    image_pos,
    proj_w,
    proj_b,
    norm_gain,
    kv_w,
    prompt_lengths,
    page_owner,
    queries,
    kv_cache,
    new_kv,
    cache_lengths,
):
    group_index = lax.axis_index("group")
    prefill = group_index == 0
    seq_index = lax.axis_index("seq")
    seq_count = lax.axis_size("seq")
    token_rows = embeds.shape[0]
    image_rows = image_feats.shape[0]
    width_local = proj_w.shape[1]
    features = gated(prefill, lambda values: values, jnp.zeros_like(image_feats), image_feats)
    spread = lax.all_to_all(features, "seq", split_axis=1, concat_axis=0, tiled=True)
    summed = lax.psum_scatter(
        gated(
            prefill,
            lambda values: jnp.dot(values, proj_w, preferred_element_type=jnp.float32),
            jnp.zeros((lax.axis_size("seq") * image_rows, width_local), jnp.float32),
            spread,
        ),
        "seq",
        scatter_dimension=0,
        tiled=True,
    )
    image_hidden = jax.nn.gelu(summed + proj_b.astype(jnp.float32), approximate=False).astype(
        jnp.bfloat16
    )
    local_pos = image_pos - seq_index * token_rows
    hidden_all = embeds.at[local_pos].set(image_hidden)
    hidden_f32 = hidden_all.astype(jnp.float32)
    squares = lax.psum(jnp.sum(hidden_f32 * hidden_f32, axis=1), "mp")
    scaled = (hidden_f32 * norm_gain.astype(jnp.float32)).astype(jnp.bfloat16)
    partial_kv = gated(
        prefill,
        lambda values: jnp.dot(values, kv_w, preferred_element_type=jnp.float32),
        jnp.zeros((token_rows, kv_w.shape[1]), jnp.float32),
        scaled,
    )
    head_kv = lax.psum_scatter(partial_kv, "mp", scatter_dimension=1, tiled=True)
    row_scale = lax.rsqrt(squares / D + 1e-05)
    positions = seq_index * token_rows + jnp.arange(token_rows, dtype=jnp.int32)
    prompt_ids = positions // PROMPT_LEN
    prompt_match = (
        prompt_ids[:, None] == jnp.arange(prompt_lengths.shape[0], dtype=jnp.int32)[None, :]
    )
    prompt_limit = jnp.sum(jnp.where(prompt_match, prompt_lengths[None, :], 0), axis=1)
    is_live = positions % PROMPT_LEN < prompt_limit
    kv_rows = jnp.where(is_live[:, None], head_kv * row_scale[:, None], 0.0).astype(jnp.bfloat16)
    page_width = kv_rows.shape[1]
    pages_dev = token_rows // PAGE
    share_pages = token_rows // PAGE
    capacity = 2 * pages_dev // seq_count
    kv_pages = kv_rows.reshape(share_pages, PAGE * page_width)
    owners = page_owner[:, 0]
    one_hot = (owners[:, None] == jnp.arange(seq_count, dtype=jnp.int32)[None, :]).astype(jnp.int32)
    page_rank = jnp.sum((jnp.cumsum(one_hot, axis=0) - one_hot) * one_hot, axis=1)
    slot_index = owners * capacity + page_rank
    selector = (
        jnp.arange(seq_count * capacity, dtype=jnp.int32)[:, None] == slot_index[None, :]
    ).astype(jnp.bfloat16)
    by_owner = jnp.dot(selector, kv_pages, preferred_element_type=jnp.float32).astype(jnp.bfloat16)
    by_owner = by_owner.reshape(seq_count * capacity, PAGE, page_width)
    block_slots = seq_count * capacity
    padded = jnp.concatenate([jnp.zeros_like(by_owner), by_owner], axis=0)
    arrived = lax.all_to_all(padded, ("group", "seq"), split_axis=0, concat_axis=0, tiled=True)
    received = arrived[:block_slots]
    page_slots = jnp.where(prefill, by_owner, received)
    empty_rows = jnp.zeros(queries.shape, jnp.bfloat16)
    attended = gated(
        jnp.logical_not(prefill), attend, empty_rows, queries, kv_cache, new_kv, cache_lengths
    )
    row_states = jnp.where(prefill, image_hidden, attended)
    return (page_slots, row_states)


def solution(mesh):
    in_specs = (
        P("seq", "mp"),
        P("seq", None),
        P("seq"),
        P("seq", "mp"),
        P("mp"),
        P("mp"),
        P("mp", None),
        P(),
        P("seq", None),
        P("seq", "mp"),
        P("seq", None, "mp"),
        P("seq", "mp"),
        P("seq"),
    )
    out_specs = (P(("group", "seq"), None, "mp"), P(("group", "seq"), "mp"))
    return jax.shard_map(
        per_device, mesh=mesh, in_specs=in_specs, out_specs=out_specs, check_vma=False
    )
```

profile of v0, /device:TPU:0, one launch (start us, length us, event | category | flops | bytes accessed | tf_op | source)
XLA Modules:
  0.0 545.2 jit_solution(15795480548592975267)
XLA Ops:
  7.2 8.3 %copy.53 = bf16[2048,2048]{1,0:T(8,128)(2,1)} copy(bf16[2048,2048]{1,0:T(8,128)(2,1)} %param.21) | data formatting | bytes 16777216
  15.4 1.5 conditional.4
  15.4 1.5 copy.44
  16.9 2.2 copy.29
  19.2 6.3 %all-to-all-start = ((bf16[128,4,1824]{0,2,1:T(8,128)(2,1)}), bf16[128,4,1824]{0,2,1:T(8,128)(2,1)S(1)}, u32[]{:S(2)}, u32[]{:S(2)}) async-start(bf16[128,4,1824]{0,2,1:T(8,128)(2,1)} %bitcast.6), calls=%async_computation | async-start | bytes 3735552 | tf_op jit(solution)/shard_map/all_to_all | solution.py:68
  25.5 0.0 reduce-scatter.3.cloned.1.call-start
  25.5 43.3 %all-to-all-done = bf16[128,4,1824]{0,2,1:T(8,128)(2,1)S(1)} async-done(((bf16[128,4,1824]{0,2,1:T(8,128)(2,1)}), bf16[128,4,1824]{0,2,1:T(8,128)(2,1)S(1)}, u32[]{:S(2)}, u32[]{:S(2)}) %all-to-all-start) | async-done | bytes 1867808 | tf_op jit(solution)/shard_map/all_to_all | solution.py:68
  68.8 0.0 copy-start.4
  68.8 0.0 copy-start.5
  68.8 0.0 copy-start.9
  68.8 12.8 %conditional.5 = (f32[512,2048]{1,0:T(8,128)}) conditional(s32[]{:T(128)} %convert_element_type.50, () %tuple.33, (bf16[4,128,1824]{1,2,0:T(8,128)(2,1)S(1)}, bf16[1824,2048]{1,0:T(8,128)(2,1)}) %tuple.61), branch_computations={%region_5.0_spmd, %region_6.0_spmd} | conditional | flops 3825205248 | bytes 17268744 | solution.py:13
  68.8 2.6 copy.30
  71.4 10.2 %fusion.46 = f32[512,2048]{1,0:T(8,128)} fusion(bf16[512,1824]{1,0:T(8,128)(2,1)} %bitcast.37, bf16[1824,2048]{1,0:T(8,128)(2,1)} %get-tuple-element.44), kind=kOutput, calls=%fused_computation.76 | convolution fusion | flops 3825205248 | bytes 13533184 | tf_op jit(solution)/shard_map/cond/branch_1_fun/dot_general | solution.py:72
  81.6 0.0 reduce-scatter.3.cloned.1.call-update
  81.6 0.0 reduce-scatter.5.cloned.1.call-start
  81.7 0.0 copy-done.4
  81.7 0.0 copy-done.5
  81.7 0.0 copy-done.9
  81.7 75.0 %reduce-scatter.3.cloned.1.call-done = f32[128,2048]{1,0:T(8,128)} async-done(((f32[512,2048]{1,0:T(8,128)}), f32[128,2048]{1,0:T(8,128)}) %reduce-scatter.3.cloned.1.call-update) | async-done | bytes 1048592 | tf_op jit(solution)/shard_map/reduce_scatter | solution.py:69
  156.7 12.6 %scatter_custom_fusion = bf16[2048,2048]{1,0:T(8,128)(2,1)} fusion(bf16[2048,2048]{1,0:T(8,128)(2,1)} %copy.53, s32[128]{0:T(128)S(1)} %compare_select_fusion.1, f32[128,2048]{1,0:T(8,128)} %reduce-scatter.3.cloned.1.call-done, f32[2048]{0:T(1024)S(1)} %convert_element_type.51), kind=kCustom, calls=%fused_computation.74 | custom fusion | flops 17301504 | bytes 9445376 | tf_op jit(solution)/shard_map/scatter | solution.py:84
  169.3 9.0 %fusion.23 = (f32[2048]{0:T(1024)S(1)}, bf16[2048,2048]{1,0:T(8,128)(2,1)}) fusion(bf16[2048,2048]{1,0:T(8,128)(2,1)} %scatter_custom_fusion, f32[2048]{0:T(1024)S(1)} %convert_element_type.54), kind=kLoop, calls=%fused_computation.27 | loop fusion | flops 20969472 | bytes 16793600 | tf_op jit(solution)/shard_map/reduce_sum | solution.py:86
  178.3 24.1 %conditional.6 = (f32[2048,2048]{1,0:T(8,128)}) conditional(s32[]{:T(128)} %convert_element_type.50, () %tuple.32, (bf16[2048,2048]{1,0:T(8,128)(2,1)}, bf16[2048,2048]{1,0:T(8,128)(2,1)}) %tuple.36), branch_computations={%region_9.0_spmd, %region_10.0_spmd} | conditional | flops 17179869184 | bytes 33554440 | solution.py:13
  178.3 24.1 %fusion.47 = f32[2048,2048]{1,0:T(8,128)} fusion(bf16[2048,2048]{1,0:T(8,128)(2,1)} %get-tuple-element.32, bf16[2048,2048]{1,0:T(8,128)(2,1)} %get-tuple-element.46), kind=kOutput, calls=%fused_computation.77 | convolution fusion | flops 17179869184 | bytes 33554432 | tf_op jit(solution)/shard_map/cond/branch_1_fun/dot_general | solution.py:90
  202.5 0.0 copy-start.6
  202.5 0.0 copy-start.7
  202.5 0.0 reduce-scatter.5.cloned.1.call-update
  202.5 0.6 copy-done.6
  203.1 0.1 fusion.35
  203.2 0.2 reduce_window_sum.11
  203.4 0.0 copy-done.7
  203.4 0.1 fusion.36
  203.5 0.2 select_reduce_fusion
  203.7 6.6 %psum.7 = f32[2048]{0:T(1024)S(1)} all-reduce(f32[2048]{0:T(1024)S(1)} %get-tuple-element.73), channel_id=1, replica_groups=mesh['group'=2,'seq'=4,'mp'=4] {'mp'}, use_global_device_ids=true, to_apply=%region_13.14 | all-reduce | flops 2048 | bytes 16384 | tf_op jit(solution)/shard_map/psum | solution.py:86
  210.3 116.8 %reduce-scatter.5.cloned.1.call-done = f32[2048,512]{1,0:T(8,128)} async-done(((f32[2048,2048]{1,0:T(8,128)}), f32[2048,512]{1,0:T(8,128)}) %reduce-scatter.5.cloned.1.call-update) | async-done | bytes 4194320 | tf_op jit(solution)/shard_map/reduce_scatter | solution.py:94
  327.1 2.6 select_convert_fusion
  329.7 2.3 reshape.94
  332.1 2.8 convolution_convert_fusion
  334.9 1.9 copy.38
  336.8 0.0 copy-start
  336.8 2.0 copy-done
  338.8 4.2 concatenate.3
  343.0 0.0 copy-start.2
  343.0 0.0 copy-start.3
  343.0 0.0 copy-start.8
  343.0 5.6 %all-to-all-start.1 = ((bf16[512,16,512]{2,1,0:T(8,128)(2,1)}), bf16[512,16,512]{2,1,0:T(8,128)(2,1)}, u32[]{:S(2)}, u32[]{:S(2)}) async-start(bf16[512,16,512]{2,1,0:T(8,128)(2,1)} %concatenate.3), calls=%async_computation.3 | async-start | bytes 16777216 | tf_op jit(solution)/shard_map/all_to_all | solution.py:120
  348.6 0.0 copy-done.2
  348.6 0.0 copy-done.3
  348.6 0.0 copy-done.8
  348.7 0.0 copy-start.1
  348.7 0.1 conditional.7
  348.7 1.1 copy-done.1
  349.9 3.1 broadcast_select_fusion
  353.0 179.5 %all-to-all-done.1 = bf16[512,16,512]{2,1,0:T(8,128)(2,1)} async-done(((bf16[512,16,512]{2,1,0:T(8,128)(2,1)}), bf16[512,16,512]{2,1,0:T(8,128)(2,1)}, u32[]{:S(2)}, u32[]{:S(2)}) %all-to-all-start.1) | async-done | bytes 8388640 | tf_op jit(solution)/shard_map/all_to_all | solution.py:120
  532.5 5.9 %slice_select_fusion = bf16[256,16,512]{2,1,0:T(8,128)(2,1)} fusion(bf16[512,16,512]{2,1,0:T(8,128)(2,1)} %all-to-all-done.1, pred[]{:T(512)S(6)} %eq.22, bf16[32,8,16,512]{3,2,1,0:T(8,128)(2,1)} %copy-done), kind=kLoop, calls=%fused_computation.29 | loop fusion | flops 2097152 | bytes 12582913 | tf_op jit(solution)/shard_map/jit(_where)/select_n | solution.py:122
  (8 shorter events, 0.1 us)
Async XLA Ops:
  19.2 49.6 %all-to-all-start = ((bf16[128,4,1824]{0,2,1:T(8,128)(2,1)}), bf16[128,4,1824]{0,2,1:T(8,128)(2,1)S(1)}, u32[]{:S(2)}, u32[]{:S(2)}) async-start(bf16[128,4,1824]{0,2,1:T(8,128)(2,1)} %bitcast.6), calls=%async_computation | async-start | bytes 3735552 | tf_op jit(solution)/shard_map/all_to_all | solution.py:68
  25.5 131.2 %reduce-scatter.3.cloned.1.call-start = ((), (), s32[]{:S(2)}) async-start(), calls=%async_computation.4 | async-start | bytes 5242880 | tf_op jit(solution)/shard_map/reduce_scatter | solution.py:69
  68.8 12.9 %copy-start.4 = (bf16[2048]{0:T(1024)(128)(2,1)S(1)}, bf16[2048]{0:T(1024)(128)(2,1)}, u32[]{:S(2)}) copy-start(bf16[2048]{0:T(1024)(128)(2,1)} %param.25) | copy-start | bytes 12292
  68.8 12.9 %copy-start.5 = (bf16[2048]{0:T(1024)(128)(2,1)S(1)}, bf16[2048]{0:T(1024)(128)(2,1)}, u32[]{:S(2)}) copy-start(bf16[2048]{0:T(1024)(128)(2,1)} %param.26) | copy-start | bytes 12292
  68.8 12.9 %copy-start.9 = (s32[128]{0:T(128)S(1)}, s32[128]{0:T(128)}, u32[]{:S(2)}) copy-start(s32[128]{0:T(128)} %param.23) | copy-start | bytes 1540
  81.6 245.5 %reduce-scatter.5.cloned.1.call-start = ((), (), s32[]{:S(2)}) async-start(), calls=%async_computation.5 | async-start | bytes 20971520 | tf_op jit(solution)/shard_map/reduce_scatter | solution.py:94
  202.5 0.7 copy-start.6
  202.5 0.9 copy-start.7
  336.8 2.0 copy-start
  343.0 5.7 %copy-start.2 = (bf16[128,2048]{1,0:T(8,128)(2,1)S(1)}, bf16[128,2048]{1,0:T(8,128)(2,1)}, u32[]{:S(2)}) copy-start(bf16[128,2048]{1,0:T(8,128)(2,1)} %param.30) | copy-start | bytes 1572868
  343.0 5.7 %copy-start.3 = (bf16[128,512]{1,0:T(8,128)(2,1)S(1)}, bf16[128,512]{1,0:T(8,128)(2,1)}, u32[]{:S(2)}) copy-start(bf16[128,512]{1,0:T(8,128)(2,1)} %param.32) | copy-start | bytes 393220
  343.0 5.7 %copy-start.8 = (s32[128]{0:T(128)S(1)}, s32[128]{0:T(128)}, u32[]{:S(2)}) copy-start(s32[128]{0:T(128)} %param.33) | copy-start | bytes 1540
  343.0 189.5 %all-to-all-start.1 = ((bf16[512,16,512]{2,1,0:T(8,128)(2,1)}), bf16[512,16,512]{2,1,0:T(8,128)(2,1)}, u32[]{:S(2)}, u32[]{:S(2)}) async-start(bf16[512,16,512]{2,1,0:T(8,128)(2,1)} %concatenate.3), calls=%async_computation.3 | async-start | bytes 16777216 | tf_op jit(solution)/shard_map/all_to_all | solution.py:120
  348.7 1.2 copy-start.1
Sparse Core Ops, SparseCore 0:
  81.7 74.9 reduce-scatter.2
  202.6 124.4 reduce-scatter.4
where the time goes:
time: 546 us; the launch traced here: 545 us
  waiting for transfers between devices  415 us (76%)
  matrix products  37.2 us (7%)
  other arithmetic  33.7 us (6%)
  local copies, waits for them, and re-layouts  26.8 us (5%)
  between operations  14.2 us (3%)
  starting transfers between devices  12 us (2%)
  blocking collectives  6.58 us (1%)
    all_to_all x1, waiting for transfers between devices, per_device(): lax.all_to_all(padded, ('group', 'seq'), split_axis=0, concat_axis=0, til...  180 us
    reduce_scatter x1, waiting for transfers between devices, per_device(): lax.psum_scatter(partial_kv, 'mp', scatter_dimension=1, tiled=True)  117 us
    reduce_scatter x1, waiting for transfers between devices, per_device(): lax.psum_scatter(gated(prefill, lambda values: jnp.dot(values, proj_w, pr...  75 us
    all_to_all x1, waiting for transfers between devices, per_device(): lax.all_to_all(features, 'seq', split_axis=1, concat_axis=0, tiled=True)  43.3 us
    dot_general x1, matrix products, per_device(): jnp.dot(values, kv_w, preferred_element_type=jnp.float32)  24.1 us
    unnamed x22, local copies, waits for them, and re-layouts  14 us
    scatter x1, other arithmetic, per_device(): hidden_all = embeds.at[local_pos].set(image_hidden)  12.6 us
  transfers between devices with their start and end apart: 4, of which 4 were waited for; matrix products, arithmetic and copies ran while one was open for 1% of the time, Pallas kernels for 0%

commit v1 on v0

v1 whole, which is shorter than its diff:
```python
import jax
import jax.numpy as jnp
from jax import lax
from jax.sharding import PartitionSpec as P

HEAD = 128
ROUTE_CHUNKS = 2


def gated(condition, action, empty_value, *operands):
    return lax.cond(condition, action, lambda *unused: empty_value, *operands)


def attend(queries, kv_cache, new_kv, cache_lengths):
    row_count = queries.shape[0]
    heads_kv = kv_cache.shape[2] // (2 * HEAD)
    grouped = queries.reshape(row_count, heads_kv, queries.shape[1] // (HEAD * heads_kv), HEAD)
    stored = kv_cache.reshape(row_count, kv_cache.shape[1], heads_kv, 2 * HEAD)
    fresh_kv = new_kv.reshape(row_count, heads_kv, 2 * HEAD)
    scores = jnp.einsum(
        "rgqh,rjgh->rgqj", grouped, stored[..., :HEAD], preferred_element_type=jnp.float32
    ) * HEAD ** (-0.5)
    in_cache = jnp.arange(stored.shape[1], dtype=jnp.int32)[None, :] < cache_lengths[:, None]
    scores = jnp.where(in_cache[:, None, None, :], scores, -1e30)
    own_score = jnp.einsum(
        "rgqh,rgh->rgq", grouped, fresh_kv[..., :HEAD], preferred_element_type=jnp.float32
    ) * HEAD ** (-0.5)
    row_max = jnp.maximum(jnp.max(scores, axis=3), own_score)
    weights = jnp.exp(scores - row_max[..., None])
    own_weight = jnp.exp(own_score - row_max)
    denominator = jnp.sum(weights, axis=3) + own_weight
    probability = (weights / denominator[..., None]).astype(jnp.bfloat16)
    own_prob = lax.optimization_barrier((own_weight / denominator).astype(jnp.bfloat16)).astype(
        jnp.float32
    )
    attended = jnp.einsum(
        "rgqj,rjgh->rgqh", probability, stored[..., HEAD:], preferred_element_type=jnp.float32
    )
    attended = attended + own_prob[..., None] * fresh_kv[:, :, None, HEAD:].astype(jnp.float32)
    return attended.astype(jnp.bfloat16).reshape(row_count, queries.shape[1])


def live_rows(positions, prompt_lengths, prompt_len):
    prompt_ids = positions // prompt_len
    match = prompt_ids[:, None] == jnp.arange(prompt_lengths.shape[0], dtype=jnp.int32)[None, :]
    limit = jnp.sum(jnp.where(match, prompt_lengths[None, :], 0), axis=1)
    return positions % prompt_len < limit


def per_device(
    embeds,
    image_feats,
    image_pos,
    proj_w,
    proj_b,
    norm_gain,
    kv_w,
    prompt_lengths,
    page_owner,
    queries,
    kv_cache,
    new_kv,
    cache_lengths,
):
    group_index = lax.axis_index("group")
    prefill = group_index == 0
    seq_index = lax.axis_index("seq")
    groups = lax.axis_size("group")
    seq_count = lax.axis_size("seq")
    mp_count = lax.axis_size("mp")
    token_rows, width_local = embeds.shape
    width = width_local * mp_count
    image_rows = image_feats.shape[0]
    prompt_len = token_rows * seq_count // prompt_lengths.shape[0]

    share_rows = image_rows // groups
    features = lax.dynamic_slice_in_dim(image_feats, group_index * share_rows, share_rows, axis=0)
    channels = proj_w.shape[0]
    shifts = [[(i, (i + k) % seq_count) for i in range(seq_count)] for k in range(seq_count)]
    pieces = [
        lax.dynamic_slice_in_dim(
            features, (seq_index + k) % seq_count * channels, channels, axis=1
        )
        for k in range(seq_count)
    ]
    pieces, norm_gain = lax.optimization_barrier((pieces, norm_gain))
    gathered = [pieces[0]]
    for k in range(1, seq_count):
        gathered.append(lax.ppermute(pieces[k], "seq", shifts[k]))
    spread = jnp.concatenate(gathered, axis=0)

    block_cols = kv_w.shape[1] // mp_count
    cols = block_cols // groups
    weight = jnp.concatenate(
        [
            lax.dynamic_slice_in_dim(kv_w, j * block_cols + group_index * cols, cols, axis=1)
            for j in range(mp_count)
        ],
        axis=1,
    )
    gain = norm_gain.astype(jnp.float32)
    text_f32 = embeds.astype(jnp.float32)
    text_scaled = (text_f32 * gain).astype(jnp.bfloat16)
    text_partial = jnp.dot(text_scaled, weight, preferred_element_type=jnp.float32)
    text_partial = text_partial.astype(jnp.bfloat16)
    text_kv = lax.psum_scatter(text_partial, "mp", scatter_dimension=1, tiled=True)
    text_squares = lax.psum(jnp.sum(text_f32 * text_f32, axis=1), "mp")

    spread, _ = lax.optimization_barrier((spread, text_partial))
    projected = jnp.dot(spread, proj_w, preferred_element_type=jnp.float32)
    projected = projected.reshape(seq_count, share_rows, width_local)
    bias, text_squares = lax.optimization_barrier((proj_b, text_squares))
    summed = projected[0] + bias.astype(jnp.float32)
    for k in range(1, seq_count):
        back = [(b, a) for a, b in shifts[k]]
        part = lax.ppermute(projected[k].astype(jnp.bfloat16), "seq", back)
        summed = summed + part.astype(jnp.float32)
    own_hidden = jax.nn.gelu(summed, approximate=False).astype(jnp.bfloat16)
    other_hidden = lax.ppermute(own_hidden, "group", [(0, 1), (1, 0)])
    image_hidden = jnp.concatenate(
        [
            jnp.where(prefill, own_hidden, other_hidden),
            jnp.where(prefill, other_hidden, own_hidden),
        ],
        axis=0,
    )

    image_f32 = image_hidden.astype(jnp.float32)
    image_scaled = (image_f32 * gain).astype(jnp.bfloat16)
    image_partial = jnp.dot(image_scaled, weight, preferred_element_type=jnp.float32)
    image_sum = jnp.sum(image_f32 * image_f32, axis=1)
    packed = jnp.concatenate(
        [
            jnp.concatenate([image_partial[:, j * cols : (j + 1) * cols] for j in range(mp_count)], axis=0),
            jnp.tile(jnp.broadcast_to(image_sum[:, None], (image_rows, HEAD)), (mp_count, 1)),
        ],
        axis=1,
    )
    packed, text_kv = lax.optimization_barrier((packed, text_kv))
    text_kv = text_kv.astype(jnp.float32)
    image_total = lax.psum_scatter(packed, "mp", scatter_dimension=0, tiled=True)
    image_scale = lax.rsqrt(image_total[:, cols] / width + 1e-05)
    image_live = live_rows(image_pos, prompt_lengths, prompt_len)
    image_kv = jnp.where(
        image_live[:, None], image_total[:, :cols] * image_scale[:, None], 0.0
    ).astype(jnp.bfloat16)

    positions = seq_index * token_rows + jnp.arange(token_rows, dtype=jnp.int32)
    is_live = live_rows(positions, prompt_lengths, prompt_len)
    placed = positions[:, None] == image_pos[None, :]
    is_image = jnp.any(placed, axis=1)
    text_scale = jnp.where(is_live, lax.rsqrt(text_squares / width + 1e-05), 0.0)
    image_part = jnp.dot(
        placed.astype(jnp.bfloat16), image_kv, preferred_element_type=jnp.float32
    )
    kv_rows = jnp.where(is_image[:, None], image_part, text_kv * text_scale[:, None]).astype(
        jnp.bfloat16
    )

    pages_dev = page_owner.shape[0]
    page = token_rows // pages_dev
    capacity = 2 * pages_dev // seq_count
    slots = seq_count * capacity
    owners = page_owner[:, 0]
    one_hot = (owners[:, None] == jnp.arange(seq_count, dtype=jnp.int32)[None, :]).astype(jnp.int32)
    page_rank = jnp.sum((jnp.cumsum(one_hot, axis=0) - one_hot) * one_hot, axis=1)
    slot_index = owners * capacity + page_rank
    selector = (jnp.arange(slots, dtype=jnp.int32)[:, None] == slot_index[None, :]).astype(
        jnp.bfloat16
    )
    step = cols // ROUTE_CHUNKS
    empty_rows = jnp.zeros(queries.shape, jnp.bfloat16)
    attended = gated(
        jnp.logical_not(prefill), attend, empty_rows, queries, kv_cache, new_kv, cache_lengths
    )
    own, other = [], []
    for chunk in range(ROUTE_CHUNKS):
        rows = kv_rows[:, chunk * step : (chunk + 1) * step].reshape(pages_dev, page * step)
        by_owner = jnp.dot(selector, rows, preferred_element_type=jnp.float32)
        by_owner = by_owner.astype(jnp.bfloat16).reshape(slots, page, step)
        arrived = lax.all_to_all(by_owner, "seq", split_axis=0, concat_axis=0, tiled=True)
        if chunk == ROUTE_CHUNKS - 1:
            arrived, attended = lax.optimization_barrier((arrived, attended))
        to_prefill = lax.ppermute(by_owner, "group", [(1, 0)])
        to_decode = lax.ppermute(arrived, "group", [(0, 1)])
        own.append(jnp.where(prefill, by_owner, arrived))
        other.append(jnp.where(prefill, to_prefill, to_decode))
    low = [jnp.where(prefill, a, b) for a, b in zip(own, other)]
    high = [jnp.where(prefill, b, a) for a, b in zip(own, other)]
    page_slots = jnp.concatenate(low + high, axis=2)

    row_states = jnp.where(prefill, image_hidden, attended)
    return (page_slots, row_states)


def solution(mesh):
    in_specs = (
        P("seq", "mp"),
        P("seq", None),
        P("seq"),
        P("seq", "mp"),
        P("mp"),
        P("mp"),
        P("mp", None),
        P(),
        P("seq", None),
        P("seq", "mp"),
        P("seq", None, "mp"),
        P("seq", "mp"),
        P("seq"),
    )
    out_specs = (P(("group", "seq"), None, "mp"), P(("group", "seq"), "mp"))
    return jax.shard_map(
        per_device, mesh=mesh, in_specs=in_specs, out_specs=out_specs, check_vma=False
    )
```

time: 546 us -> 263 us (0.48)
  waiting for transfers between devices: 415 us -> 115 us
  starting transfers between devices: 12 us -> 74.4 us
  other arithmetic: 33.7 us -> 15.1 us
  local copies, waits for them, and re-layouts: 26.8 us -> 11.2 us
  matrix products: 37.2 us -> 24 us
    all_to_all x2, waiting for transfers between devices: 223 us -> 23.7 us  [per_device(): lax.all_to_all(by_owner, 'seq', split_axis=0, concat_axis=0, tiled=True)]
    reduce_scatter x2, waiting for transfers between devices: 192 us -> 23 us  [the longest x1 23 us: per_device(): lax.psum_scatter(packed, 'mp', scatter_dimension=0, tiled=True)]
    ppermute x0 -> x11, waiting for transfers between devices: none -> 68.2 us  [the longest x2 29.6 us: per_device(): to_prefill = lax.ppermute(by_owner, 'group', [(1, 0)])]
    ppermute x0 -> x11, starting transfers between devices: none -> 66.2 us  [the longest x2 47.8 us: per_device(): to_decode = lax.ppermute(arrived, 'group', [(0, 1)])]
    dot_general x3 -> x6, matrix products: 37.2 us -> 24 us  [the longest x1 10.9 us: per_device(): jnp.dot(text_scaled, weight, preferred_element_type=jnp.float32)]
    scatter x1 -> x0, other arithmetic: 12.6 us -> none  [per_device(): hidden_all = embeds.at[local_pos].set(image_hidden)]
    unnamed x22 -> x24, local copies, waits for them, and re-layouts: 14 us -> 5.25 us
    reduce_sum x2 -> x4, other arithmetic: 9.12 us -> 2.06 us  [the longest x1 1.7 us: per_device(): text_squares = lax.psum(jnp.sum(text_f32 * text_f32, axis=1), 'mp')]
  transfers between devices with their start and end apart: 4 -> 15, of which waited for: 4 -> 11; matrix products, arithmetic and copies ran while one was open for 1% -> 8% of each run, Pallas kernels for 0% -> 0%
where the time goes in v1:
time: 263 us; the launch traced here: 262 us
  waiting for transfers between devices  115 us (44%)
  starting transfers between devices  74.4 us (28%)
  matrix products  24 us (9%)
  other arithmetic  15.1 us (6%)
  between operations  14.5 us (6%)
  local copies, waits for them, and re-layouts  11.2 us (4%)
  blocking collectives  7.39 us (3%)
    ppermute x2, starting transfers between devices, per_device(): to_decode = lax.ppermute(arrived, 'group', [(0, 1)])  47.8 us
    ppermute x2, waiting for transfers between devices, per_device(): to_prefill = lax.ppermute(by_owner, 'group', [(1, 0)])  29.6 us
    all_to_all x2, waiting for transfers between devices, per_device(): lax.all_to_all(by_owner, 'seq', split_axis=0, concat_axis=0, tiled=True)  23.7 us
    reduce_scatter x1, waiting for transfers between devices, per_device(): lax.psum_scatter(packed, 'mp', scatter_dimension=0, tiled=True)  23 us
    ppermute x3, waiting for transfers between devices, per_device(): gathered.append(lax.ppermute(pieces[k], 'seq', shifts[k]))  14.7 us
    ppermute x3, waiting for transfers between devices, per_device(): part = lax.ppermute(projected[k].astype(jnp.bfloat16), 'seq', back)  14.1 us
    dot_general x1, matrix products, per_device(): jnp.dot(text_scaled, weight, preferred_element_type=jnp.float32)  10.9 us
    all_to_all x2, starting transfers between devices, per_device(): lax.all_to_all(by_owner, 'seq', split_axis=0, concat_axis=0, tiled=True)  8.1 us
  transfers between devices with their start and end apart: 15, of which 11 were waited for; matrix products, arithmetic and copies ran while one was open for 8% of the time, Pallas kernels for 0%

profile of v1, /device:TPU:0, one launch (start us, length us, event | category | flops | bytes accessed | tf_op | source)
XLA Modules:
  0.0 261.5 jit_solution(16297288117892525210)
XLA Ops:
  7.2 0.0 reduce-scatter.3.cloned.1.call-start
  7.3 1.8 fusion.79
  9.1 0.7 convert_element_type.77
  9.8 2.6 %constant_dynamic-slice_fusion.3 = (bf16[2048,256]{1,0:T(8,128)(2,1)S(1)}, bf16[2048,256]{1,0:T(8,128)(2,1)S(1)}, bf16[2048,256]{1,0:T(8,128)(2,1)S(1)}, bf16[2048,256]{1,0:T(8,128)(2,1)S(1)}) fusion(bf16[2048,2048]{1,0:T(8,128)(2,1)} %param.21, s32[]{:T(128)S(6)} %select_n.181, s32[]{:T(128)S(6)} %select_n.182, s32[]{:T(128)S(6)} %select_n.184, ...), kind=kLoop, calls=%fused_computation.128 | loop fusion | bytes 8388624 | tf_op jit(solution)/shard_map/dynamic_slice | solution.py:96
  12.4 1.0 copy-done.1
  13.4 0.3 copy-done.2
  13.8 1.5 copy-done
  15.2 10.9 %fusion.27 = bf16[2048,1024]{1,0:T(8,128)(2,1)} fusion(bf16[2048,2048]{1,0:T(8,128)(2,1)S(1)} %copy-done, f32[2048]{0:T(1024)S(1)} %convert_element_type.77, bf16[2048,256]{1,0:T(8,128)(2,1)S(1)} %get-tuple-element.65, bf16[2048,256]{1,0:T(8,128)(2,1)S(1)} %get-tuple-element.66, bf16[2048,256]{1,0:T(8,128)(2,1)S(1)} %get-tuple-element.64, ...), kind=kOutput, calls=%fused_computation.31 | convolution fusion | flops 8621391872 | bytes 16785408 | tf_op jit(solution)/shard_map/dot_general | solution.py:104
  26.2 0.0 reduce-scatter.3.cloned.1.call-update
  26.2 0.0 reduce-scatter.5.cloned.1.call-start
  26.2 3.1 %collective-permute-start = (bf16[64,1824]{1,0:T(8,128)(2,1)S(1)}, bf16[64,1824]{1,0:T(8,128)(2,1)S(1)}, u32[]{:S(2)}, u32[]{:S(2)}) collective-permute-start(bf16[64,1824]{1,0:T(8,128)(2,1)S(1)} %get-tuple-element.30), channel_id=1, source_target_pairs={{0,4},{4,8},{8,12},{12,0},{1,5},{5,9},{9,13},{13,1},{2,6},{6,10},{... | collective-permute-start | bytes 700424 | tf_op jit(solution)/shard_map/ppermute | solution.py:89
  29.3 2.6 collective-permute-start.1
  31.9 1.3 collective-permute-start.2
  33.3 5.0 %collective-permute-done = bf16[64,1824]{1,0:T(8,128)(2,1)S(1)} collective-permute-done((bf16[64,1824]{1,0:T(8,128)(2,1)S(1)}, bf16[64,1824]{1,0:T(8,128)(2,1)S(1)}, u32[]{:S(2)}, u32[]{:S(2)}) %collective-permute-start) | collective-permute-done | bytes 233504 | tf_op jit(solution)/shard_map/ppermute | solution.py:89
  38.3 9.7 %collective-permute-done.1 = bf16[64,1824]{1,0:T(8,128)(2,1)S(1)} collective-permute-done((bf16[64,1824]{1,0:T(8,128)(2,1)S(1)}, bf16[64,1824]{1,0:T(8,128)(2,1)S(1)}, u32[]{:S(2)}, u32[]{:S(2)}) %collective-permute-start.1) | collective-permute-done | bytes 233504 | tf_op jit(solution)/shard_map/ppermute | solution.py:89
  48.0 0.1 pad_maximum_fusion.2
  48.1 7.0 %fusion.83 = (bf16[256,2048]{1,0:T(8,128)(2,1)S(1)}, f32[256,2048]{1,0:T(8,128)}) fusion(bf16[256,1824]{1,0:T(8,128)(2,1)S(1)} %pad_maximum_fusion.2, bf16[1824,2048]{1,0:T(8,128)(2,1)} %param.18), kind=kOutput, calls=%fused_computation.139 | convolution fusion | flops 1913126912 | bytes 11550720 | tf_op jit(solution)/shard_map/dot_general | solution.py:110
  55.2 0.8 fusion.81
  55.9 6.7 %collective-permute-start.3 = (bf16[64,2048]{1,0:T(8,128)(2,1)}, bf16[64,2048]{1,0:T(8,128)(2,1)S(1)}, u32[]{:S(2)}, u32[]{:S(2)}) collective-permute-start(bf16[64,2048]{1,0:T(8,128)(2,1)} %get-tuple-element.77), channel_id=1, source_target_pairs={{4,0},{8,4},{12,8},{0,12},{5,1},{9,5},{13,9},{1,13},{6,2},{10,6},{... | collective-permute-start | bytes 786440 | tf_op jit(solution)/shard_map/ppermute | solution.py:116
  62.7 0.6 collective-permute-start.4
  63.3 1.7 fusion.23
  65.0 7.4 %psum.7 = f32[2048]{0:T(1024)S(1)} all-reduce(f32[2048]{0:T(1024)S(1)} %fusion.23), channel_id=1, replica_groups=mesh['group'=2,'seq'=4,'mp'=4] {'mp'}, use_global_device_ids=true, to_apply=%region_5.6 | all-reduce | flops 2048 | bytes 16384 | tf_op jit(solution)/shard_map/psum | solution.py:107
  72.4 3.4 %collective-permute-done.5 = bf16[64,2048]{1,0:T(8,128)(2,1)S(1)} collective-permute-done((bf16[64,2048]{1,0:T(8,128)(2,1)S(1)}, bf16[64,2048]{1,0:T(8,128)(2,1)S(1)}, u32[]{:S(2)}, u32[]{:S(2)}) %collective-permute-start.5) | collective-permute-done | bytes 262176 | tf_op jit(solution)/shard_map/ppermute | solution.py:116
  75.8 10.7 %collective-permute-done.4 = bf16[64,2048]{1,0:T(8,128)(2,1)S(1)} collective-permute-done((bf16[64,2048]{1,0:T(8,128)(2,1)S(1)}, bf16[64,2048]{1,0:T(8,128)(2,1)S(1)}, u32[]{:S(2)}, u32[]{:S(2)}) %collective-permute-start.4) | collective-permute-done | bytes 262176 | tf_op jit(solution)/shard_map/ppermute | solution.py:116
  86.5 2.3 fusion.39
  88.8 1.5 collective-permute-start.6
  90.3 0.1 fusion.64
  90.4 0.2 reduce_window_sum.11
  90.6 5.7 %collective-permute-done.6 = bf16[64,2048]{1,0:T(8,128)(2,1)S(1)} collective-permute-done((bf16[64,2048]{1,0:T(8,128)(2,1)S(1)}, bf16[64,2048]{1,0:T(8,128)(2,1)S(1)}, u32[]{:S(2)}, u32[]{:S(2)}) %collective-permute-start.6) | collective-permute-done | bytes 262176 | tf_op jit(solution)/shard_map/ppermute | solution.py:119
  96.4 0.2 fusion.35
  96.6 3.0 %fusion.36 = f32[128,1024]{1,0:T(8,128)S(1)} fusion(bf16[2048,256]{1,0:T(8,128)(2,1)} %copy-done.1, bf16[2048,256]{1,0:T(8,128)(2,1)} %copy-done.2, bf16[2048,256]{1,0:T(8,128)(2,1)S(1)} %get-tuple-element.64, bf16[2048,256]{1,0:T(8,128)(2,1)S(1)} %get-tuple-element.63, f32[2048]{0:T(1024)S(1)} %convert_element_type.77, ...), kind=kOutput, calls=%fused_computation.55 | convolution fusion | flops 555220992 | bytes 5251072 | tf_op jit(solution)/shard_map/dot_general | solution.py:130
  99.6 0.1 tile.13
  99.8 0.9 pad_maximum_fusion.3
  100.7 0.0 reduce-scatter.5.cloned.1.call-update
  100.8 0.1 fusion.73
  100.9 0.1 fusion.66
  101.0 0.2 select_reduce_fusion
  101.2 0.6 compare_reduce_fusion
  101.8 23.0 %reduce-scatter.5.cloned.1.call-done = f32[128,384]{1,0:T(8,128)} async-done(((f32[512,384]{1,0:T(8,128)}), f32[128,384]{1,0:T(8,128)}) %reduce-scatter.5.cloned.1.call-update) | async-done | bytes 196624 | tf_op jit(solution)/shard_map/reduce_scatter | solution.py:141
  124.8 0.9 fusion.59
  125.8 2.2 fusion.30
  128.0 0.1 fusion.80
  128.1 0.2 reshape.102
  128.3 0.4 fusion.32
  128.7 1.2 copy.32
  130.0 4.6 %all-to-all-start.1 = ((bf16[256,16,128]{2,1,0:T(8,128)(2,1)}), bf16[256,16,128]{2,1,0:T(8,128)(2,1)S(1)}, u32[]{:S(2)}, u32[]{:S(2)}) async-start(bf16[256,16,128]{2,1,0:T(8,128)(2,1)} %bitcast.15), calls=%async_computation.3 | async-start | bytes 2097152 | tf_op jit(solution)/shard_map/all_to_all | solution.py:181
  134.5 0.2 reshape.100
  134.8 0.4 fusion.31
  135.2 1.2 copy.31
  136.4 23.7 %all-to-all-done.1 = bf16[256,16,128]{2,1,0:T(8,128)(2,1)S(1)} async-done(((bf16[256,16,128]{2,1,0:T(8,128)(2,1)}), bf16[256,16,128]{2,1,0:T(8,128)(2,1)S(1)}, u32[]{:S(2)}, u32[]{:S(2)}) %all-to-all-start.1) | async-done | bytes 1048608 | tf_op jit(solution)/shard_map/all_to_all | solution.py:181
  160.1 3.5 %all-to-all-start = ((bf16[256,16,128]{2,1,0:T(8,128)(2,1)}), bf16[256,16,128]{2,1,0:T(8,128)(2,1)S(1)}, u32[]{:S(2)}, u32[]{:S(2)}) async-start(bf16[256,16,128]{2,1,0:T(8,128)(2,1)} %bitcast.13), calls=%async_computation.2 | async-start | bytes 2097152 | tf_op jit(solution)/shard_map/all_to_all | solution.py:181
  163.7 0.1 conditional.1
  163.7 1.3 collective-permute-start.9
  165.0 42.2 %collective-permute-start.10 = (bf16[256,16,128]{2,1,0:T(8,128)(2,1)S(1)}, bf16[256,16,128]{2,1,0:T(8,128)(2,1)}, u32[]{:S(2)}, u32[]{:S(2)}) collective-permute-start(bf16[256,16,128]{2,1,0:T(8,128)(2,1)S(1)} %all-to-all-done.1), channel_id=1, source_target_pairs={{0,16},{1,17},{2,18},{3,19},{4,20},{5,21},{6,22},{7,23},{8,24},{9,... | collective-permute-start | bytes 3145736 | tf_op jit(solution)/shard_map/ppermute | solution.py:185
  207.2 1.3 collective-permute-start.7
  208.5 5.6 %collective-permute-start.8 = (bf16[256,16,128]{2,1,0:T(8,128)(2,1)S(1)}, bf16[256,16,128]{2,1,0:T(8,128)(2,1)S(1)}, u32[]{:S(2)}, u32[]{:S(2)}) collective-permute-start(bf16[256,16,128]{2,1,0:T(8,128)(2,1)S(1)} %all-to-all-done), channel_id=1, source_target_pairs={{0,16},{1,17},{2,18},{3,19},{4,20},{5,21},{6,22},{7,23},{8,24},{9,... | collective-permute-start | bytes 3145736 | tf_op jit(solution)/shard_map/ppermute | solution.py:185
  214.1 0.9 broadcast_select_fusion.8
  215.0 12.6 %collective-permute-done.9 = bf16[256,16,128]{2,1,0:T(8,128)(2,1)} collective-permute-done((bf16[256,16,128]{2,1,0:T(8,128)(2,1)}, bf16[256,16,128]{2,1,0:T(8,128)(2,1)}, u32[]{:S(2)}, u32[]{:S(2)}) %collective-permute-start.9) | collective-permute-done | bytes 1048608 | tf_op jit(solution)/shard_map/ppermute | solution.py:184
  227.6 2.2 collective-permute-done.10
  229.8 1.8 broadcast_select_fusion.2
  231.6 17.0 %collective-permute-done.7 = bf16[256,16,128]{2,1,0:T(8,128)(2,1)} collective-permute-done((bf16[256,16,128]{2,1,0:T(8,128)(2,1)}, bf16[256,16,128]{2,1,0:T(8,128)(2,1)}, u32[]{:S(2)}, u32[]{:S(2)}) %collective-permute-start.7) | collective-permute-done | bytes 1048608 | tf_op jit(solution)/shard_map/ppermute | solution.py:184
  248.5 1.9 collective-permute-done.8
  250.4 1.9 broadcast_select_fusion.5
  252.3 2.3 pad_maximum_fusion.1
  (36 shorter events, 0.3 us)
Async XLA Ops:
  7.2 93.5 %reduce-scatter.3.cloned.1.call-start = ((), (), s32[]{:S(2)}) async-start(), calls=%async_computation.4 | async-start | bytes 5242880 | tf_op jit(solution)/shard_map/reduce_scatter | solution.py:106
  9.8 5.5 %copy-start = (bf16[2048,2048]{1,0:T(8,128)(2,1)S(1)}, bf16[2048,2048]{1,0:T(8,128)(2,1)}, u32[]{:S(2)}) copy-start(bf16[2048,2048]{1,0:T(8,128)(2,1)} %param.15) | copy-start | bytes 25165828
  12.4 1.0 copy-start.1
  12.4 1.3 copy-start.2
  26.2 98.6 %reduce-scatter.5.cloned.1.call-start = ((), (), s32[]{:S(2)}) async-start(), calls=%async_computation.5 | async-start | bytes 983040 | tf_op jit(solution)/shard_map/reduce_scatter | solution.py:141
  26.2 12.1 %collective-permute-start = (bf16[64,1824]{1,0:T(8,128)(2,1)S(1)}, bf16[64,1824]{1,0:T(8,128)(2,1)S(1)}, u32[]{:S(2)}, u32[]{:S(2)}) collective-permute-start(bf16[64,1824]{1,0:T(8,128)(2,1)S(1)} %get-tuple-element.30), channel_id=1, source_target_pairs={{0,4},{4,8},{8,12},{12,0},{1,5},{5,9},{9,13},{13,1},{2,6},{6,10},{... | collective-permute-start | bytes 700424 | tf_op jit(solution)/shard_map/ppermute | solution.py:89
  29.3 18.7 %collective-permute-start.1 = (bf16[64,1824]{1,0:T(8,128)(2,1)S(1)}, bf16[64,1824]{1,0:T(8,128)(2,1)S(1)}, u32[]{:S(2)}, u32[]{:S(2)}) collective-permute-start(bf16[64,1824]{1,0:T(8,128)(2,1)S(1)} %get-tuple-element.31), channel_id=1, source_target_pairs={{0,8},{4,12},{8,0},{12,4},{1,9},{5,13},{9,1},{13,5},{2,10},{6,14},... | collective-permute-start | bytes 700424 | tf_op jit(solution)/shard_map/ppermute | solution.py:89
  31.9 16.1 %collective-permute-start.2 = (bf16[64,1824]{1,0:T(8,128)(2,1)S(1)}, bf16[64,1824]{1,0:T(8,128)(2,1)S(1)}, u32[]{:S(2)}, u32[]{:S(2)}) collective-permute-start(bf16[64,1824]{1,0:T(8,128)(2,1)S(1)} %get-tuple-element.32), channel_id=1, source_target_pairs={{0,12},{4,0},{8,4},{12,8},{1,13},{5,1},{9,5},{13,9},{2,14},{6,2},{... | collective-permute-start | bytes 700424 | tf_op jit(solution)/shard_map/ppermute | solution.py:89
  48.0 15.2 %slice-start = ((s8[8388608]{0:T(1024)(128)(4,1)}), s8[4194304]{0:T(1024)(128)(4,1)S(1)}, s32[]{:S(2)}) async-start(s8[8388608]{0:T(1024)(128)(4,1)} %bitcast.35), calls=%async_computation.6 | async-start | bytes 8388608
  48.1 15.2 %slice-start.1 = ((s8[8388608]{0:T(1024)(128)(4,1)}), s8[4194304]{0:T(1024)(128)(4,1)S(1)}, s32[]{:S(2)}) async-start(s8[8388608]{0:T(1024)(128)(4,1)} %bitcast.35), calls=%async_computation.7 | async-start | bytes 8388608
  55.2 17.2 %copy-start.4 = (bf16[2048]{0:T(1024)(128)(2,1)S(1)}, bf16[2048]{0:T(1024)(128)(2,1)}, u32[]{:S(2)}) copy-start(bf16[2048]{0:T(1024)(128)(2,1)} %param.19) | copy-start | bytes 12292
  55.2 35.1 %copy-start.5 = (s32[128,1]{0,1:T(1,128)S(1)}, s32[128,1]{0,1:T(1,128)}, u32[]{:S(2)}) copy-start(s32[128,1]{0,1:T(1,128)} %param.23) | copy-start | bytes 1540
  55.9 16.4 %collective-permute-start.3 = (bf16[64,2048]{1,0:T(8,128)(2,1)}, bf16[64,2048]{1,0:T(8,128)(2,1)S(1)}, u32[]{:S(2)}, u32[]{:S(2)}) collective-permute-start(bf16[64,2048]{1,0:T(8,128)(2,1)} %get-tuple-element.77), channel_id=1, source_target_pairs={{4,0},{8,4},{12,8},{0,12},{5,1},{9,5},{13,9},{1,13},{6,2},{10,6},{... | collective-permute-start | bytes 786440 | tf_op jit(solution)/shard_map/ppermute | solution.py:116
  62.7 13.1 %collective-permute-start.5 = (bf16[64,2048]{1,0:T(8,128)(2,1)S(1)}, bf16[64,2048]{1,0:T(8,128)(2,1)S(1)}, u32[]{:S(2)}, u32[]{:S(2)}) collective-permute-start(bf16[64,2048]{1,0:T(8,128)(2,1)S(1)} %get-tuple-element.78), channel_id=1, source_target_pairs={{12,0},{0,4},{4,8},{8,12},{13,1},{1,5},{5,9},{9,13},{14,2},{2,6},{... | collective-permute-start | bytes 786440 | tf_op jit(solution)/shard_map/ppermute | solution.py:116
  62.7 23.8 %collective-permute-start.4 = (bf16[64,2048]{1,0:T(8,128)(2,1)S(1)}, bf16[64,2048]{1,0:T(8,128)(2,1)S(1)}, u32[]{:S(2)}, u32[]{:S(2)}) collective-permute-start(bf16[64,2048]{1,0:T(8,128)(2,1)S(1)} %get-tuple-element.79), channel_id=1, source_target_pairs={{8,0},{12,4},{0,8},{4,12},{9,1},{13,5},{1,9},{5,13},{10,2},{14,6},... | collective-permute-start | bytes 786440 | tf_op jit(solution)/shard_map/ppermute | solution.py:116
  88.8 7.5 %collective-permute-start.6 = (bf16[64,2048]{1,0:T(8,128)(2,1)S(1)}, bf16[64,2048]{1,0:T(8,128)(2,1)S(1)}, u32[]{:S(2)}, u32[]{:S(2)}) collective-permute-start(bf16[64,2048]{1,0:T(8,128)(2,1)S(1)} %fusion.39), channel_id=1, source_target_pairs={{0,16},{16,0},{1,17},{17,1},{2,18},{18,2},{3,19},{19,3},{4,20},{20... | collective-permute-start | bytes 786440 | tf_op jit(solution)/shard_map/ppermute | solution.py:119
  96.5 4.2 %copy-start.8 = (s32[128]{0:T(128)S(1)}, s32[128]{0:T(128)}, u32[]{:S(2)}) copy-start(s32[128]{0:T(128)} %param.17) | copy-start | bytes 1540
  96.6 4.2 %copy-start.6 = (s32[2]{0:T(128)S(1)}, s32[2]{0:T(128)}, u32[]{:S(2)}) copy-start(s32[2]{0:T(128)} %param.22) | copy-start | bytes 28
  128.0 35.7 %copy-start.3 = (bf16[128,512]{1,0:T(8,128)(2,1)S(1)}, bf16[128,512]{1,0:T(8,128)(2,1)}, u32[]{:S(2)}) copy-start(bf16[128,512]{1,0:T(8,128)(2,1)} %param.26) | copy-start | bytes 393220
  128.0 35.7 %copy-start.7 = (s32[128]{0:T(128)S(1)}, s32[128]{0:T(128)}, u32[]{:S(2)}) copy-start(s32[128]{0:T(128)} %param.27) | copy-start | bytes 1540
  130.0 30.2 %all-to-all-start.1 = ((bf16[256,16,128]{2,1,0:T(8,128)(2,1)}), bf16[256,16,128]{2,1,0:T(8,128)(2,1)S(1)}, u32[]{:S(2)}, u32[]{:S(2)}) async-start(bf16[256,16,128]{2,1,0:T(8,128)(2,1)} %bitcast.15), calls=%async_computation.3 | async-start | bytes 2097152 | tf_op jit(solution)/shard_map/all_to_all | solution.py:181
  160.1 48.4 %all-to-all-start = ((bf16[256,16,128]{2,1,0:T(8,128)(2,1)}), bf16[256,16,128]{2,1,0:T(8,128)(2,1)S(1)}, u32[]{:S(2)}, u32[]{:S(2)}) async-start(bf16[256,16,128]{2,1,0:T(8,128)(2,1)} %bitcast.13), calls=%async_computation.2 | async-start | bytes 2097152 | tf_op jit(solution)/shard_map/all_to_all | solution.py:181
  163.7 63.9 %collective-permute-start.9 = (bf16[256,16,128]{2,1,0:T(8,128)(2,1)}, bf16[256,16,128]{2,1,0:T(8,128)(2,1)}, u32[]{:S(2)}, u32[]{:S(2)}) collective-permute-start(bf16[256,16,128]{2,1,0:T(8,128)(2,1)} %bitcast.15), channel_id=1, source_target_pairs={{16,0},{17,1},{18,2},{19,3},{20,4},{21,5},{22,6},{23,7},{24,8},{25... | collective-permute-start | bytes 3145736 | tf_op jit(solution)/shard_map/ppermute | solution.py:184
  165.0 64.8 %collective-permute-start.10 = (bf16[256,16,128]{2,1,0:T(8,128)(2,1)S(1)}, bf16[256,16,128]{2,1,0:T(8,128)(2,1)}, u32[]{:S(2)}, u32[]{:S(2)}) collective-permute-start(bf16[256,16,128]{2,1,0:T(8,128)(2,1)S(1)} %all-to-all-done.1), channel_id=1, source_target_pairs={{0,16},{1,17},{2,18},{3,19},{4,20},{5,21},{6,22},{7,23},{8,24},{9,... | collective-permute-start | bytes 3145736 | tf_op jit(solution)/shard_map/ppermute | solution.py:185
  207.2 41.3 %collective-permute-start.7 = (bf16[256,16,128]{2,1,0:T(8,128)(2,1)}, bf16[256,16,128]{2,1,0:T(8,128)(2,1)}, u32[]{:S(2)}, u32[]{:S(2)}) collective-permute-start(bf16[256,16,128]{2,1,0:T(8,128)(2,1)} %bitcast.13), channel_id=1, source_target_pairs={{16,0},{17,1},{18,2},{19,3},{20,4},{21,5},{22,6},{23,7},{24,8},{25... | collective-permute-start | bytes 3145736 | tf_op jit(solution)/shard_map/ppermute | solution.py:184
  208.5 41.9 %collective-permute-start.8 = (bf16[256,16,128]{2,1,0:T(8,128)(2,1)S(1)}, bf16[256,16,128]{2,1,0:T(8,128)(2,1)S(1)}, u32[]{:S(2)}, u32[]{:S(2)}) collective-permute-start(bf16[256,16,128]{2,1,0:T(8,128)(2,1)S(1)} %all-to-all-done), channel_id=1, source_target_pairs={{0,16},{1,17},{2,18},{3,19},{4,20},{5,21},{6,22},{7,23},{8,24},{9,... | collective-permute-start | bytes 3145736 | tf_op jit(solution)/shard_map/ppermute | solution.py:185
Sparse Core Ops, SparseCore 0:
  26.3 47.3 reduce-scatter.2
  100.9 23.9 reduce-scatter.4
